TPU v7x, 32 devices: a whole 2x2x4 slice. The times are simulated.
32 devices in a mesh: tm: 8 (over y, x, core), grp: 4 (over z).
Axes of the slice: x: 2, y: 2, z: 4, core: 2. Of those that a mesh axis runs over, the one named last changes fastest.
Arguments:
- series: float32 [131072, 512], P(('tm', 'grp')), may hold values from -6 to 6
- filter_taps: float32 [33], replicated, may hold values from -1 to 1
- sign_flips: int32 [131072], P(('tm', 'grp')), may hold values from -1 to 1, as said below
- samples: int32 [8192], replicated, may hold values from 0 to 131071, as said below
Outputs:
- sketch: float32 [8192, 512], P(('tm', 'grp'))
- r_factor: float32 [512, 512], replicated
Inputs may be any that keep to these rules, and one draw needn't show every extreme that they name: `sign_flips`: each entry is -1 or +1. All distinct; the values of samples modulo 4096 take exactly 4096 distinct values, each by exactly 2 consecutive entries; entries are ordered by their value modulo 4096, then by value.
All inputs are finite; a program needn't handle non-finite values.
Results may differ from a plain program's by a relative error of at most 0.0003.
Values sent between devices are 32-bit elements; how exact they have to be, the bound alone decides.
A program may use at most 128 MiB of HBM per device.

v0:
```python
import jax
import jax.numpy as jnp
from jax import lax
from jax.sharding import PartitionSpec as P


def extended(block, sides, width):
    for axis, dim in sides:
        count = lax.axis_size(axis)
        forward = [(i, i + 1) for i in range(count - 1)]
        backward = [(target, source) for source, target in forward]
        low = lax.ppermute(
            lax.slice_in_dim(block, block.shape[dim] - width, None, axis=dim), axis, forward
        )
        high = lax.ppermute(lax.slice_in_dim(block, 0, width, axis=dim), axis, backward)
        block = jnp.concatenate([low, block, high], axis=dim)
    return block


def bit_count(values, width_bits):
    counted = jnp.zeros_like(values)
    for offset in range(width_bits):
        counted = counted + (values >> offset & 1)
    return counted


def hadamard(order):
    row_ids = jnp.arange(order, dtype=jnp.int32)[:, None]
    col_ids = jnp.arange(order, dtype=jnp.int32)[None, :]
    parity = bit_count(row_ids & col_ids, max(order.bit_length(), 1)) & 1
    return (1 - 2 * parity).astype(jnp.float32)


def local_transform(rows_block):
    length, columns = rows_block.shape
    levels = length.bit_length() - 1
    outer = 2 ** ((levels + 1) // 2)
    inner = length // outer
    layered = rows_block.reshape(outer, inner, columns)
    layered = jnp.einsum("ux,xvw->uvw", hadamard(outer), layered, precision=lax.Precision.HIGHEST)
    layered = jnp.einsum("vy,uyw->uvw", hadamard(inner), layered, precision=lax.Precision.HIGHEST)
    return layered.reshape(length, columns)


def on_device(series, filter_taps, sign_flips, samples):
    rows_dev = series.shape[0]
    columns = series.shape[1]
    tap_count = filter_taps.shape[0]
    half_taps = (tap_count - 1) // 2
    devices_all = lax.axis_size("tm") * lax.axis_size("grp")
    total_rows = rows_dev * devices_all
    sample_count = samples.shape[0]
    padded = extended(series, ((("tm", "grp"), 0),), half_taps)
    filtered = filter_taps[0] * padded[0:rows_dev]
    for offset in range(1, tap_count):
        filtered = filtered + filter_taps[offset] * padded[offset : offset + rows_dev]
    flipped = filtered * sign_flips.astype(jnp.float32)[:, None]
    mixed = local_transform(flipped)
    position = lax.axis_index("tm") * lax.axis_size("grp") + lax.axis_index("grp")
    row_scale = 1.0 / jnp.sqrt(jnp.float32(total_rows))
    block_rows = sample_count // devices_all
    copies = max(2, sample_count // rows_dev)
    distinct = sample_count // copies
    per_device = distinct // devices_all
    used_positions = samples[::copies] % rows_dev
    outgoing = jnp.take(mixed, used_positions, axis=0)
    incoming = lax.all_to_all(outgoing, ("tm", "grp"), split_axis=0, concat_axis=0, tiled=True)
    stacked = incoming.reshape(devices_all, per_device, columns)
    combined = (
        jnp.einsum("op,pkw->okw", hadamard(devices_all), stacked, precision=lax.Precision.HIGHEST)
        * row_scale
    )
    combined = combined.reshape(devices_all * per_device, columns)
    mine = lax.dynamic_slice_in_dim(samples, position * block_rows, block_rows)
    slot_index = mine // rows_dev * per_device + jnp.arange(block_rows, dtype=jnp.int32) // copies
    sketch = jnp.take(combined, slot_index, axis=0)
    local_gram = lax.dot_general(
        sketch,
        sketch,
        (((0,), (0,)), ((), ())),
        precision=lax.Precision.HIGHEST,
        preferred_element_type=jnp.float32,
    )
    gram = lax.psum(local_gram, ("tm", "grp"))
    lower = jnp.linalg.cholesky(gram / sample_count)
    return (sketch, lower.T)


def solution(mesh):
    return jax.shard_map(
        on_device,
        mesh=mesh,
        in_specs=(P(("tm", "grp"), None), P(), P(("tm", "grp")), P()),
        out_specs=(P(("tm", "grp"), None), P()),
        check_vma=False,
    )
```

profile of v0, /device:TPU:0, one launch (start us, length us, event | category | flops | bytes accessed | tf_op | source)
XLA Modules:
  0.0 659.5 jit_solution(13701622514079241855)
XLA Ops:
  7.9 4.9 collective-permute-start
  15.6 2.1 fusion.111
  17.7 1.9 fusion.112
  20.9 11.5 %constant_dynamic-update-slice_fusion = (f32[4112,512]{1,0:T(8,128)}, f32[4112,512]{1,0:T(8,128)}) fusion(f32[4112,512]{1,0:T(8,128)} %constant_dynamic-update-slice_fusion.1, f32[4096,512]{1,0:T(8,128)} %param.4), kind=kLoop, calls=%fused_computation.143 | loop fusion | bytes 25165824 | tf_op jit(solution)/shard_map/concatenate | solution.py:16
  33.0 122.8 %fusion.1 = f32[4096,512]{1,0:T(8,128)S(1)} fusion(f32[4112,512]{1,0:T(8,128)} %constant_dynamic-update-slice_fusion.2, f32[4112,512]{1,0:T(8,128)} %get-tuple-element.10, f32[4096,512]{1,0:T(8,128)} %param.4, f32[4096]{0:T(1024)S(1)} %convert_element_type.14, f32[]{:T(128)} %bitcast.35, f32[]{:T(128)} %bitcast.34, f32[]{:T(128)} %bitcast.33, f32[]{:T(128)} %bitcast.32, ...), kind=kLoop, calls=%fused_computation.4 | loop fusion | flops 138412032 | bytes 285229184 | tf_op jit(solution)/shard_map/mul | solution.py:57
  155.8 12.4 %fusion.37 = f32[64,64,512]{2,0,1:T(8,128)S(1)} fusion(f32[64,64,512]{2,1,0:T(8,128)S(1)} %bitcast.77), kind=kOutput, calls=%fused_computation.71 | convolution fusion | flops 1610715136 | bytes 16777216 | tf_op jit(solution)/shard_map/ux,xvw->uvw/dot_general | solution.py:40
  168.3 13.8 %fusion.35 = f32[64,512,64]{1,2,0:T(8,128)} fusion(f32[64,64,512]{2,0,1:T(8,128)S(1)} %fusion.37), kind=kOutput, calls=%fused_computation.69 | convolution fusion | flops 1610715136 | bytes 16777216 | tf_op jit(solution)/shard_map/vy,uyw->uvw/dot_general | solution.py:41
  182.1 21.4 %gather_fusion = f32[4096,512]{1,0:T(8,128)} fusion(f32[4096,512]{1,0:T(8,128)} %bitcast.75, s32[4096]{0:T(1024)S(1)} %broadcast_clamp_fusion), kind=kCustom, calls=%fused_computation | custom fusion | bytes 16793600 | tf_op jit(solution)/shard_map/jit(_take)/gather | solution.py:66
  203.5 5.8 broadcast_select_fusion
  209.3 7.0 %all-to-all-start = ((f32[32,128,512]{2,1,0:T(8,128)}), f32[32,128,512]{2,1,0:T(8,128)}, u32[]{:S(2)}, u32[]{:S(2)}) async-start(f32[32,128,512]{2,1,0:T(8,128)} %broadcast_select_fusion), calls=%async_computation | async-start | bytes 16777216 | tf_op jit(solution)/shard_map/all_to_all | solution.py:67
  217.2 180.5 %all-to-all-done = f32[32,128,512]{2,1,0:T(8,128)} async-done(((f32[32,128,512]{2,1,0:T(8,128)}), f32[32,128,512]{2,1,0:T(8,128)}, u32[]{:S(2)}, u32[]{:S(2)}) %all-to-all-start) | async-done | bytes 8388640 | tf_op jit(solution)/shard_map/all_to_all | solution.py:67
  397.7 16.9 %broadcast_multiply_fusion = f32[32,128,512]{2,0,1:T(8,128)S(1)} fusion(f32[32,128,512]{2,1,0:T(8,128)} %all-to-all-done), kind=kOutput, calls=%fused_computation.73 | convolution fusion | flops 807426048 | bytes 16777216 | tf_op jit(solution)/shard_map/op,pkw->okw/dot_general | solution.py:70
  414.6 8.1 %copy.18 = f32[32,128,512]{2,1,0:T(8,128)} copy(f32[32,128,512]{2,0,1:T(8,128)S(1)} %broadcast_multiply_fusion) | data formatting | bytes 16777216 | tf_op jit(solution)/shard_map/mul | solution.py:70
  422.7 4.6 gather_fusion.1
  427.4 2.0 fusion.113
  429.4 134.7 %all-reduce.3.cloned.1.call-done = f32[512,512]{0,1:T(8,128)} async-done(((f32[512,512]{0,1:T(8,128)}), f32[512,512]{0,1:T(8,128)}) %all-reduce.3.cloned.1.call-update) | async-done | bytes 1048592 | tf_op jit(solution)/shard_map/psum | solution.py:84
  565.8 1.5 fusion.41
  567.3 11.7 %cholesky.104 = f32[128,128]{1,0:T(8,128)S(1)} custom-call(f32[128,128]{1,0:T(8,128)S(1)} %cholesky.266), custom_call_target="Cholesky" | custom-call | tf_op jit(solution)/shard_map/jit(cholesky)/cholesky | solution.py:85
  579.2 10.0 %custom-call.27 = f32[1,128,128]{1,2,0:T(8,128)S(1)} custom-call(f32[1,128,128]{2,1,0:T(8,128)S(1)} %get-tuple-element.23), custom_call_target="InvertDiagBlocksLowerTriangular" | custom-call | tf_op jit(solution)/shard_map/jit(cholesky)/cholesky | solution.py:85
  589.8 11.7 %cholesky.217 = f32[128,128]{1,0:T(8,128)S(1)} custom-call(f32[128,128]{1,0:T(8,128)S(1)} %cholesky.270), custom_call_target="Cholesky" | custom-call | tf_op jit(solution)/shard_map/jit(cholesky)/cholesky | solution.py:85
  601.6 9.8 %custom-call.28 = f32[1,128,128]{1,2,0:T(8,128)S(1)} custom-call(f32[1,128,128]{2,1,0:T(8,128)S(1)} %get-tuple-element.20), custom_call_target="InvertDiagBlocksLowerTriangular" | custom-call | tf_op jit(solution)/shard_map/jit(cholesky)/cholesky | solution.py:85
  612.1 11.9 %cholesky.238 = f32[128,128]{1,0:T(8,128)S(1)} custom-call(f32[128,128]{1,0:T(8,128)S(1)} %cholesky.275), custom_call_target="Cholesky" | custom-call | tf_op jit(solution)/shard_map/jit(cholesky)/cholesky | solution.py:85
  624.0 9.8 %custom-call.29 = f32[1,128,128]{1,2,0:T(8,128)S(1)} custom-call(f32[1,128,128]{2,1,0:T(8,128)S(1)} %get-tuple-element.17), custom_call_target="InvertDiagBlocksLowerTriangular" | custom-call | tf_op jit(solution)/shard_map/jit(cholesky)/cholesky | solution.py:85
  634.5 11.7 %cholesky.255 = f32[128,128]{1,0:T(8,128)S(1)} custom-call(f32[128,128]{1,0:T(8,128)S(1)} %convolution_subtract_fusion.2), custom_call_target="Cholesky" | custom-call | tf_op jit(solution)/shard_map/jit(cholesky)/cholesky | solution.py:85
  (38 shorter events, 13.6 us)
Async XLA Ops:
  7.9 12.4 %collective-permute-start = (f32[16,512]{1,0:T(8,128)S(1)}, f32[16,512]{1,0:T(8,128)S(1)}, u32[]{:S(2)}, u32[]{:S(2)}) collective-permute-start(f32[16,512]{1,0:T(8,128)S(1)} %get-tuple-element.12), channel_id=1, source_target_pairs={{0,1},{1,2},{2,3},{3,4},{4,5},{5,6},{6,7},{7,8},{8,9},{9,10},{10,1... | collective-permute-start | bytes 98312 | tf_op jit(solution)/shard_map/ppermute | solution.py:12
  12.9 19.5 %collective-permute-start.1 = (f32[16,512]{1,0:T(8,128)S(1)}, f32[16,512]{1,0:T(8,128)S(1)}, u32[]{:S(2)}, u32[]{:S(2)}) collective-permute-start(f32[16,512]{1,0:T(8,128)S(1)} %get-tuple-element.13), channel_id=1, source_target_pairs={{1,0},{2,1},{3,2},{4,3},{5,4},{6,5},{7,6},{8,7},{9,8},{10,9},{11,1... | collective-permute-start | bytes 98312 | tf_op jit(solution)/shard_map/ppermute | solution.py:15
  209.3 188.4 %all-to-all-start = ((f32[32,128,512]{2,1,0:T(8,128)}), f32[32,128,512]{2,1,0:T(8,128)}, u32[]{:S(2)}, u32[]{:S(2)}) async-start(f32[32,128,512]{2,1,0:T(8,128)} %broadcast_select_fusion), calls=%async_computation | async-start | bytes 16777216 | tf_op jit(solution)/shard_map/all_to_all | solution.py:67
  216.3 347.8 %all-reduce.3.cloned.1.call-start = ((), (), s32[]{:S(2)}) async-start(), calls=%async_computation.1 | async-start | bytes 2097152 | tf_op jit(solution)/shard_map/psum | solution.py:84
  427.4 223.5 %copy-start = (f32[256,512]{1,0:T(8,128)}, f32[256,512]{1,0:T(8,128)S(1)}, u32[]{:S(2)}) copy-start(f32[256,512]{1,0:T(8,128)S(1)} %broadcast_select_fusion.1) | copy-start | bytes 1572868
Sparse Core Ops, SparseCore 0:
  429.5 134.5 all-reduce.2
where the time goes:
time: 664 us; the launch traced here: 659 us
  waiting for transfers between devices  315 us (47%)
  other arithmetic  212 us (32%)
  local copies, waits for them, and re-layouts  54.7 us (8%)
  matrix products  47 us (7%)
  between operations  17.3 us (3%)
  starting transfers between devices  13.3 us (2%)
    all_to_all x1, waiting for transfers between devices, on_device(): lax.all_to_all(outgoing, ('tm', 'grp'), split_axis=0, concat_axis=0, tile...  181 us
    psum x1, waiting for transfers between devices, on_device(): gram = lax.psum(local_gram, ('tm', 'grp'))  135 us
    mul x1, other arithmetic, on_device(): flipped = filtered * sign_flips.astype(jnp.float32)[:, None]  123 us
    another operation x14, other arithmetic, on_device(): lower = jnp.linalg.cholesky(gram / sample_count)  78.8 us
    gather x1, local copies, waits for them, and re-layouts, on_device(): outgoing = jnp.take(mixed, used_positions, axis=0)  21.4 us
    dot_general x1, matrix products, on_device(): jnp.einsum('op,pkw->okw', hadamard(devices_all), stacked, precision=lax.P...  16.9 us
    dot_general x1, matrix products, local_transform(): jnp.einsum('vy,uyw->uvw', hadamard(inner), layered, precision=lax.Precisi...  13.8 us
  transfers between devices with their start and end apart: 4, of which 2 were waited for; matrix products, arithmetic and copies ran while one was open for 3% of the time, Pallas kernels for 0%

commit v1 on v0

--- a/solution.py
+++ b/solution.py
@@ -81,7 +81,8 @@
         precision=lax.Precision.HIGHEST,
         preferred_element_type=jnp.float32,
     )
-    gram = lax.psum(local_gram, ("tm", "grp"))
+    one_axis = lax.psum(local_gram, "grp")
+    gram = lax.psum(one_axis, "tm")
     lower = jnp.linalg.cholesky(gram / sample_count)
     return (sketch, lower.T)
 

time: 664 us -> 645 us (0.971)
  waiting for transfers between devices: 315 us -> 295 us
    psum x1 -> x2, waiting for transfers between devices: 135 us -> 115 us  [the longest x1 59.1 us: on_device(): gram = lax.psum(one_axis, 'tm')]
  transfers between devices with their start and end apart: 4 -> 5, of which waited for: 2 -> 3; matrix products, arithmetic and copies ran while one was open for 3% -> 3% of each run, Pallas kernels for 0% -> 0%
where the time goes in v1:
time: 645 us; the launch traced here: 640 us
  waiting for transfers between devices  295 us (46%)
  other arithmetic  212 us (33%)
  local copies, waits for them, and re-layouts  54.7 us (8%)
  matrix products  47.2 us (7%)
  between operations  17.3 us (3%)
  starting transfers between devices  13.6 us (2%)
    all_to_all x1, waiting for transfers between devices, on_device(): lax.all_to_all(outgoing, ('tm', 'grp'), split_axis=0, concat_axis=0, tile...  181 us
    mul x1, other arithmetic, on_device(): flipped = filtered * sign_flips.astype(jnp.float32)[:, None]  123 us
    another operation x14, other arithmetic, on_device(): lower = jnp.linalg.cholesky(gram / sample_count)  78.6 us
    psum x1, waiting for transfers between devices, on_device(): gram = lax.psum(one_axis, 'tm')  59.1 us
    psum x1, waiting for transfers between devices, on_device(): one_axis = lax.psum(local_gram, 'grp')  55.6 us
    gather x1, local copies, waits for them, and re-layouts, on_device(): outgoing = jnp.take(mixed, used_positions, axis=0)  21.4 us
    dot_general x1, matrix products, on_device(): jnp.einsum('op,pkw->okw', hadamard(devices_all), stacked, precision=lax.P...  17.3 us
    dot_general x1, matrix products, local_transform(): jnp.einsum('vy,uyw->uvw', hadamard(inner), layered, precision=lax.Precisi...  13.6 us
  transfers between devices with their start and end apart: 5, of which 3 were waited for; matrix products, arithmetic and copies ran while one was open for 3% of the time, Pallas kernels for 0%

profile of v1, /device:TPU:0, one launch (start us, length us, event | category | flops | bytes accessed | tf_op | source)
XLA Modules:
  0.0 639.8 jit_solution(9243776003949060286)
XLA Ops:
  7.9 4.9 collective-permute-start
  15.6 2.1 fusion.111
  17.7 1.9 fusion.112
  20.9 11.5 %constant_dynamic-update-slice_fusion = (f32[4112,512]{1,0:T(8,128)}, f32[4112,512]{1,0:T(8,128)}) fusion(f32[4112,512]{1,0:T(8,128)} %constant_dynamic-update-slice_fusion.1, f32[4096,512]{1,0:T(8,128)} %param.4), kind=kLoop, calls=%fused_computation.143 | loop fusion | bytes 25165824 | tf_op jit(solution)/shard_map/concatenate | solution.py:16
  33.0 122.8 %fusion.1 = f32[4096,512]{1,0:T(8,128)S(1)} fusion(f32[4112,512]{1,0:T(8,128)} %constant_dynamic-update-slice_fusion.2, f32[4112,512]{1,0:T(8,128)} %get-tuple-element.10, f32[4096,512]{1,0:T(8,128)} %param.4, f32[4096]{0:T(1024)S(1)} %convert_element_type.14, f32[]{:T(128)} %bitcast.35, f32[]{:T(128)} %bitcast.34, f32[]{:T(128)} %bitcast.33, f32[]{:T(128)} %bitcast.32, ...), kind=kLoop, calls=%fused_computation.4 | loop fusion | flops 138412032 | bytes 285229184 | tf_op jit(solution)/shard_map/mul | solution.py:57
  155.8 12.4 %fusion.37 = f32[64,64,512]{2,0,1:T(8,128)S(1)} fusion(f32[64,64,512]{2,1,0:T(8,128)S(1)} %bitcast.77), kind=kOutput, calls=%fused_computation.71 | convolution fusion | flops 1610715136 | bytes 16777216 | tf_op jit(solution)/shard_map/ux,xvw->uvw/dot_general | solution.py:40
  168.3 13.6 %fusion.35 = f32[64,512,64]{1,2,0:T(8,128)} fusion(f32[64,64,512]{2,0,1:T(8,128)S(1)} %fusion.37), kind=kOutput, calls=%fused_computation.69 | convolution fusion | flops 1610715136 | bytes 16777216 | tf_op jit(solution)/shard_map/vy,uyw->uvw/dot_general | solution.py:41
  181.8 21.4 %gather_fusion = f32[4096,512]{1,0:T(8,128)} fusion(f32[4096,512]{1,0:T(8,128)} %bitcast.75, s32[4096]{0:T(1024)S(1)} %broadcast_clamp_fusion), kind=kCustom, calls=%fused_computation | custom fusion | bytes 16793600 | tf_op jit(solution)/shard_map/jit(_take)/gather | solution.py:66
  203.3 5.8 broadcast_select_fusion
  209.1 7.0 %all-to-all-start = ((f32[32,128,512]{2,1,0:T(8,128)}), f32[32,128,512]{2,1,0:T(8,128)}, u32[]{:S(2)}, u32[]{:S(2)}) async-start(f32[32,128,512]{2,1,0:T(8,128)} %broadcast_select_fusion), calls=%async_computation | async-start | bytes 16777216 | tf_op jit(solution)/shard_map/all_to_all | solution.py:67
  217.0 180.5 %all-to-all-done = f32[32,128,512]{2,1,0:T(8,128)} async-done(((f32[32,128,512]{2,1,0:T(8,128)}), f32[32,128,512]{2,1,0:T(8,128)}, u32[]{:S(2)}, u32[]{:S(2)}) %all-to-all-start) | async-done | bytes 8388640 | tf_op jit(solution)/shard_map/all_to_all | solution.py:67
  397.5 17.3 %broadcast_multiply_fusion = f32[32,128,512]{2,0,1:T(8,128)S(1)} fusion(f32[32,128,512]{2,1,0:T(8,128)} %all-to-all-done), kind=kOutput, calls=%fused_computation.73 | convolution fusion | flops 807426048 | bytes 16777216 | tf_op jit(solution)/shard_map/op,pkw->okw/dot_general | solution.py:70
  414.8 8.1 %copy.18 = f32[32,128,512]{2,1,0:T(8,128)} copy(f32[32,128,512]{2,0,1:T(8,128)S(1)} %broadcast_multiply_fusion) | data formatting | bytes 16777216 | tf_op jit(solution)/shard_map/mul | solution.py:70
  422.9 4.6 gather_fusion.1
  427.6 2.0 fusion.113
  429.9 55.6 %all-reduce.4.cloned.1.call-done = f32[512,512]{0,1:T(8,128)} async-done(((f32[512,512]{0,1:T(8,128)}), f32[512,512]{0,1:T(8,128)}) %all-reduce.4.cloned.1.call-update) | async-done | bytes 1048592 | tf_op jit(solution)/shard_map/psum | solution.py:84
  485.5 59.1 %all-reduce.6.cloned.1.call-done = f32[512,512]{0,1:T(8,128)} async-done(((f32[512,512]{0,1:T(8,128)}), f32[512,512]{0,1:T(8,128)}) %all-reduce.6.cloned.1.call-update) | async-done | bytes 1048592 | tf_op jit(solution)/shard_map/psum | solution.py:85
  547.8 11.7 %cholesky.104 = f32[128,128]{1,0:T(8,128)S(1)} custom-call(f32[128,128]{1,0:T(8,128)S(1)} %cholesky.266), custom_call_target="Cholesky" | custom-call | tf_op jit(solution)/shard_map/jit(cholesky)/cholesky | solution.py:86
  559.7 9.8 %custom-call.27 = f32[1,128,128]{1,2,0:T(8,128)S(1)} custom-call(f32[1,128,128]{2,1,0:T(8,128)S(1)} %get-tuple-element.23), custom_call_target="InvertDiagBlocksLowerTriangular" | custom-call | tf_op jit(solution)/shard_map/jit(cholesky)/cholesky | solution.py:86
  570.1 11.7 %cholesky.217 = f32[128,128]{1,0:T(8,128)S(1)} custom-call(f32[128,128]{1,0:T(8,128)S(1)} %cholesky.270), custom_call_target="Cholesky" | custom-call | tf_op jit(solution)/shard_map/jit(cholesky)/cholesky | solution.py:86
  581.9 10.0 %custom-call.28 = f32[1,128,128]{1,2,0:T(8,128)S(1)} custom-call(f32[1,128,128]{2,1,0:T(8,128)S(1)} %get-tuple-element.20), custom_call_target="InvertDiagBlocksLowerTriangular" | custom-call | tf_op jit(solution)/shard_map/jit(cholesky)/cholesky | solution.py:86
  592.6 11.7 %cholesky.238 = f32[128,128]{1,0:T(8,128)S(1)} custom-call(f32[128,128]{1,0:T(8,128)S(1)} %cholesky.275), custom_call_target="Cholesky" | custom-call | tf_op jit(solution)/shard_map/jit(cholesky)/cholesky | solution.py:86
  604.3 9.8 %custom-call.29 = f32[1,128,128]{1,2,0:T(8,128)S(1)} custom-call(f32[1,128,128]{2,1,0:T(8,128)S(1)} %get-tuple-element.17), custom_call_target="InvertDiagBlocksLowerTriangular" | custom-call | tf_op jit(solution)/shard_map/jit(cholesky)/cholesky | solution.py:86
  614.8 11.7 %cholesky.255 = f32[128,128]{1,0:T(8,128)S(1)} custom-call(f32[128,128]{1,0:T(8,128)S(1)} %convolution_subtract_fusion.2), custom_call_target="Cholesky" | custom-call | tf_op jit(solution)/shard_map/jit(cholesky)/cholesky | solution.py:86
  (41 shorter events, 15.3 us)
Async XLA Ops:
  7.9 12.4 %collective-permute-start = (f32[16,512]{1,0:T(8,128)S(1)}, f32[16,512]{1,0:T(8,128)S(1)}, u32[]{:S(2)}, u32[]{:S(2)}) collective-permute-start(f32[16,512]{1,0:T(8,128)S(1)} %get-tuple-element.12), channel_id=1, source_target_pairs={{0,1},{1,2},{2,3},{3,4},{4,5},{5,6},{6,7},{7,8},{8,9},{9,10},{10,1... | collective-permute-start | bytes 98312 | tf_op jit(solution)/shard_map/ppermute | solution.py:12
  12.9 19.5 %collective-permute-start.1 = (f32[16,512]{1,0:T(8,128)S(1)}, f32[16,512]{1,0:T(8,128)S(1)}, u32[]{:S(2)}, u32[]{:S(2)}) collective-permute-start(f32[16,512]{1,0:T(8,128)S(1)} %get-tuple-element.13), channel_id=1, source_target_pairs={{1,0},{2,1},{3,2},{4,3},{5,4},{6,5},{7,6},{8,7},{9,8},{10,9},{11,1... | collective-permute-start | bytes 98312 | tf_op jit(solution)/shard_map/ppermute | solution.py:15
  209.1 188.4 %all-to-all-start = ((f32[32,128,512]{2,1,0:T(8,128)}), f32[32,128,512]{2,1,0:T(8,128)}, u32[]{:S(2)}, u32[]{:S(2)}) async-start(f32[32,128,512]{2,1,0:T(8,128)} %broadcast_select_fusion), calls=%async_computation | async-start | bytes 16777216 | tf_op jit(solution)/shard_map/all_to_all | solution.py:67
  216.1 269.3 %all-reduce.4.cloned.1.call-start = ((), (), s32[]{:S(2)}) async-start(), calls=%async_computation.1 | async-start | bytes 2097152 | tf_op jit(solution)/shard_map/psum | solution.py:84
  427.6 203.6 %copy-start = (f32[256,512]{1,0:T(8,128)}, f32[256,512]{1,0:T(8,128)S(1)}, u32[]{:S(2)}) copy-start(f32[256,512]{1,0:T(8,128)S(1)} %broadcast_select_fusion.1) | copy-start | bytes 1572868
  429.7 115.0 %all-reduce.6.cloned.1.call-start = ((), (), s32[]{:S(2)}) async-start(), calls=%async_computation.2 | async-start | bytes 2097152 | tf_op jit(solution)/shard_map/psum | solution.py:85
Sparse Core Ops, SparseCore 0:
  429.8 55.6 all-reduce.3
  488.6 55.9 all-reduce.5
